TPU v7x, 128 devices: a whole 4x4x4 slice. The times are simulated.
128 devices in a mesh: sample: 8 (over y_hi, z), landmark: 16 (over y_lo, x, core).
Axes of the slice: x: 4, y: 4 (y_hi: 2, y_lo: 2; y = y_hi * 2 + y_lo), z: 4, core: 2. Of those that a mesh axis runs over, the one named last changes fastest.
Arguments:
- embeddings: bfloat16 [8192, 4096], P('sample'), may hold values from -6 to 6
- landmarks: bfloat16 [16384, 4096], P('landmark'), may hold values from -6 to 6
- factor: bfloat16 [16384, 16384], P('landmark', 'sample')
- flips: int32 [512, 8192], P(None, 'sample'), may hold values from 0 to 1
- labels: int32 [8192], P('sample'), may hold values from 0 to 1, as said below
- counts: int32 [8], replicated, may hold values from 256 to 1024, as said below
Outputs:
- whitened: bfloat16 [16384, 512], P(('sample', 'landmark'))
- statistic: float32 [512], replicated
Inputs may be any that keep to these rules, and one draw needn't show every extreme that they name: `counts`: one slab holds exactly 1024 live rows. `labels`: 0 or 1; the first slot of every slab is of corpus 0 and the second of corpus 1.
All inputs are finite; a program needn't handle non-finite values.
Results may differ from a plain program's by a relative error of at most 0.029.
Values may be sent and summed in bfloat16 or wider, within the bound.
A program may use at most 128 MiB of HBM per device.

v0:
```python
import math
import jax
import jax.numpy as jnp
from jax import lax
from jax.sharding import PartitionSpec as P

D = 4096
LANDMARKS = 16384


def whiten_maker(factor, moments_half):
    return lax.dot_general(
        factor, moments_half, (((0,), (1,)), ((), ())), preferred_element_type=jnp.float32
    )


def local(embeddings, landmarks, factor, flips, labels, counts):
    slot_count = embeddings.shape[0]
    slab_total = counts.shape[0]
    here_index = lax.axis_index("sample")
    own_count = jnp.sum(jnp.where(jnp.arange(slab_total, dtype=jnp.int32) == here_index, counts, 0))
    live_rows = (jnp.arange(slot_count, dtype=jnp.int32) < own_count).astype(jnp.float32)
    corpus = labels.astype(jnp.float32)
    count_a, count_b = lax.psum(
        (jnp.sum(live_rows * (1.0 - corpus)), jnp.sum(live_rows * corpus)), "sample"
    )
    balance = jnp.sqrt(count_a * count_b / (count_a + count_b))
    row_weight = live_rows * ((1.0 - corpus) / count_a - corpus / count_b) * balance
    wide_x = embeddings.astype(jnp.float32)
    row_scale = lax.rsqrt(jnp.mean(wide_x * wide_x, axis=1) + 1e-06)
    wide_z = landmarks.astype(jnp.float32)
    point_scale = lax.rsqrt(jnp.mean(wide_z * wide_z, axis=1) + 1e-06)
    signs = (2 * flips - 1).astype(jnp.bfloat16)
    cross = lax.dot_general(
        embeddings, landmarks, (((1,), (1,)), ((), ())), preferred_element_type=jnp.float32
    )
    kern = jnp.exp(0.5 * cross * row_scale[:, None] * point_scale[None, :] / math.sqrt(D))
    weighted = (row_weight[:, None] * kern).astype(jnp.bfloat16)
    partial_value = jnp.dot(signs, weighted, preferred_element_type=jnp.float32)
    summed = lax.psum(partial_value.astype(jnp.bfloat16), "sample")
    wide = lax.psum_scatter(
        whiten_maker(factor, summed).astype(jnp.bfloat16),
        "landmark",
        scatter_dimension=0,
        tiled=True,
    ).astype(jnp.float32)
    share = jnp.sum(wide * wide, axis=0)
    statistic = lax.psum(share, ("sample", "landmark")) / LANDMARKS
    return (wide.astype(jnp.bfloat16), statistic)


def solution(mesh):
    return jax.shard_map(
        local,
        mesh=mesh,
        in_specs=(
            P("sample", None),
            P("landmark", None),
            P("landmark", "sample"),
            P(None, "sample"),
            P("sample"),
            P(),
        ),
        out_specs=(P(("sample", "landmark"), None), P()),
        check_vma=False,
    )
```

profile of v0, /device:TPU:1, one launch (start us, length us, event | category | flops | bytes accessed | tf_op | source)
XLA Modules:
  0.0 293.1 jit_solution(10554155324927165992)
XLA Ops:
  7.2 0.0 all-reduce.3.cloned.1.call-start
  7.2 1.3 fusion.9
  8.5 2.0 select_reduce_fusion
  10.5 23.3 %all-reduce = (f32[]{:T(128)}, f32[]{:T(128)}) all-reduce(f32[]{:T(128)} %get-tuple-element.7, f32[]{:T(128)} %get-tuple-element.6), channel_id=1, replica_groups=mesh['sample'=8,'landmark'=16] {'sample'}, use_global_device_ids=true, to_apply=%region_2.3 | all-reduce | flops 2 | bytes 16 | tf_op jit(solution)/shard_map/psum | solution.py:24
  36.3 2.5 select_multiply_fusion
  38.9 0.0 copy-start
  38.9 5.2 %multiply_reduce_fusion.1 = f32[1024]{0:T(1024)S(1)} fusion(bf16[1024,4096]{1,0:T(8,128)(2,1)} %param.6), kind=kLoop, calls=%fused_computation.1 | loop fusion | flops 12581888 | bytes 8392704 | tf_op jit(solution)/shard_map/reduce_sum | solution.py:30
  44.1 0.5 copy-done
  44.7 0.0 copy-start.1
  44.7 1.7 multiply_reduce_fusion
  46.4 0.0 copy-done.1
  46.4 16.2 %fusion.6 = bf16[512,1024]{1,0:T(8,128)(2,1)} fusion(bf16[1024,4096]{1,0:T(8,128)(2,1)} %param.6, bf16[1024,4096]{1,0:T(8,128)(2,1)} %param.7, f32[1024]{0:T(1024)S(1)} %get-tuple-element.10, f32[1024]{0:T(1024)S(1)} %get-tuple-element.11, f32[1024]{0:T(1024)S(1)} %select_multiply_fusion, s32[512,1024]{1,0:T(8,128)S(1)} %copy-done.1), kind=kOutput, calls=%fused_computation.11 | convolution fusion | flops 9671016448 | bytes 19935232 | tf_op jit(solution)/shard_map/dot_general | solution.py:39
  62.6 0.0 all-reduce.3.cloned.1.call-update
  62.6 0.0 reduce-scatter.4.cloned.1.call-start
  62.7 83.6 %all-reduce.3.cloned.1.call-done = bf16[512,1024]{1,0:T(8,128)(2,1)} async-done(((bf16[512,1024]{1,0:T(8,128)(2,1)}), bf16[512,1024]{1,0:T(8,128)(2,1)}) %all-reduce.3.cloned.1.call-update) | async-done | bytes 1048592 | tf_op jit(solution)/shard_map/psum | solution.py:40
  146.3 4.8 %fusion = bf16[2048,512]{0,1:T(8,128)(2,1)S(1)} fusion(bf16[512,1024]{1,0:T(8,128)(2,1)} %all-reduce.3.cloned.1.call-done, bf16[1024,2048]{1,0:T(8,128)(2,1)} %param.8), kind=kOutput, calls=%fused_computation.4 | convolution fusion | flops 2148532224 | bytes 7340032 | tf_op jit(solution)/shard_map/dot_general | solution.py:12
  151.1 2.5 copy.10
  153.6 0.0 reduce-scatter.4.cloned.1.call-update
  153.7 62.8 %reduce-scatter.4.cloned.1.call-done = bf16[128,512]{1,0:T(8,128)(2,1)} async-done(((bf16[2048,512]{1,0:T(8,128)(2,1)}), bf16[128,512]{1,0:T(8,128)(2,1)}) %reduce-scatter.4.cloned.1.call-update) | async-done | bytes 131088
  216.4 1.0 copy.11
  217.4 0.2 multiply_reduce_fusion.2
  217.6 68.1 %psum.31 = f32[512]{0:T(512)S(1)} all-reduce(f32[512]{0:T(512)S(1)} %multiply_reduce_fusion.2), channel_id=1, replica_groups=mesh['sample'=8,'landmark'=16] {'sample','landmark'}, use_global_device_ids=true, to_apply=%region_10.11 | all-reduce | flops 512 | bytes 4096 | tf_op jit(solution)/shard_map/psum | solution.py:48
  285.7 0.6 broadcast_multiply_fusion
  (1 shorter events, 0.0 us)
Async XLA Ops:
  7.2 139.1 %all-reduce.3.cloned.1.call-start = ((), (), s32[]{:S(2)}) async-start(), calls=%async_computation.1 | async-start | bytes 2097152 | tf_op jit(solution)/shard_map/psum | solution.py:40
  38.9 5.8 %copy-start = (bf16[1024,4096]{1,0:T(8,128)(2,1)S(1)}, bf16[1024,4096]{1,0:T(8,128)(2,1)}, u32[]{:S(2)}) copy-start(bf16[1024,4096]{1,0:T(8,128)(2,1)} %param.7) | copy-start | bytes 25165828
  44.7 1.7 copy-start.1
  62.6 153.8 %reduce-scatter.4.cloned.1.call-start = ((), (), s32[]{:S(2)}) async-start(), calls=%async_computation.2 | async-start | bytes 2228224
Sparse Core Ops, SparseCore 0:
  62.7 83.4 all-reduce.2
  153.8 62.5 reduce-scatter.3
where the time goes:
time: 293 us
  waiting for transfers between devices  146 us (50%)
  blocking collectives  91.4 us (31%)
  matrix products  21.1 us (7%)
  between operations  16.6 us (6%)
  other arithmetic  13.5 us (5%)
  local copies, waits for them, and re-layouts  4.09 us (1%)
    psum x1, waiting for transfers between devices, local(): summed = lax.psum(partial_value.astype(jnp.bfloat16), 'sample')  83.6 us
    psum x1, blocking collectives, local(): statistic = lax.psum(share, ('sample', 'landmark')) / LANDMARKS  68.1 us
    unnamed x3, waiting for transfers between devices  62.8 us
    psum x1, blocking collectives, local(): lax.psum((jnp.sum(live_rows * (1.0 - corpus)), jnp.sum(live_rows * corpus...  23.3 us
    dot_general x1, matrix products, local(): partial_value = jnp.dot(signs, weighted, preferred_element_type=jnp.float32)  16.2 us
  transfers between devices with their start and end apart: 2, of which 2 were waited for; matrix products, arithmetic and copies ran while one was open for 0% of the time, Pallas kernels for 0%

commit v1 on v0

--- a/solution.py
+++ b/solution.py
@@ -45,7 +45,7 @@
         tiled=True,
     ).astype(jnp.float32)
     share = jnp.sum(wide * wide, axis=0)
-    statistic = lax.psum(share, ("sample", "landmark")) / LANDMARKS
+    statistic = lax.psum(lax.psum(share, "landmark"), "sample") / LANDMARKS
     return (wide.astype(jnp.bfloat16), statistic)
 
 

time: 293 us -> 280 us (0.956); the launches traced: 293 us -> 276 us
  blocking collectives: 91.4 us -> 74.4 us
    psum x1 -> x2, blocking collectives: 68.1 us -> 51.1 us  [local(): statistic = lax.psum(lax.psum(share, 'landmark'), 'sample') / LANDMARKS]
where the time goes in v1:
time: 280 us; the launch traced here: 276 us
  waiting for transfers between devices  146 us (52%)
  blocking collectives  74.4 us (27%)
  matrix products  21.1 us (8%)
  between operations  16.6 us (6%)
  other arithmetic  13.5 us (5%)
  local copies, waits for them, and re-layouts  4.09 us (1%)
    psum x1, waiting for transfers between devices, local(): summed = lax.psum(partial_value.astype(jnp.bfloat16), 'sample')  83.6 us
    unnamed x3, waiting for transfers between devices  62.8 us
    psum x2, blocking collectives, local(): statistic = lax.psum(lax.psum(share, 'landmark'), 'sample') / LANDMARKS  51.1 us
    psum x1, blocking collectives, local(): lax.psum((jnp.sum(live_rows * (1.0 - corpus)), jnp.sum(live_rows * corpus...  23.3 us
    dot_general x1, matrix products, local(): partial_value = jnp.dot(signs, weighted, preferred_element_type=jnp.float32)  16.2 us
  transfers between devices with their start and end apart: 2, of which 2 were waited for; matrix products, arithmetic and copies ran while one was open for 0% of the time, Pallas kernels for 0%

profile of v1, /device:TPU:1, one launch (start us, length us, event | category | flops | bytes accessed | tf_op | source)
XLA Modules:
  0.0 276.1 jit_solution(13844982850213343633)
XLA Ops:
  7.2 0.0 all-reduce.3.cloned.1.call-start
  7.2 1.3 fusion.9
  8.5 2.0 select_reduce_fusion
  10.5 23.3 %all-reduce = (f32[]{:T(128)}, f32[]{:T(128)}) all-reduce(f32[]{:T(128)} %get-tuple-element.7, f32[]{:T(128)} %get-tuple-element.6), channel_id=1, replica_groups=mesh['sample'=8,'landmark'=16] {'sample'}, use_global_device_ids=true, to_apply=%region_2.3 | all-reduce | flops 2 | bytes 16 | tf_op jit(solution)/shard_map/psum | solution.py:24
  36.3 2.5 select_multiply_fusion
  38.9 0.0 copy-start
  38.9 5.2 %multiply_reduce_fusion.1 = f32[1024]{0:T(1024)S(1)} fusion(bf16[1024,4096]{1,0:T(8,128)(2,1)} %param.6), kind=kLoop, calls=%fused_computation.1 | loop fusion | flops 12581888 | bytes 8392704 | tf_op jit(solution)/shard_map/reduce_sum | solution.py:30
  44.1 0.5 copy-done
  44.7 0.0 copy-start.1
  44.7 1.7 multiply_reduce_fusion
  46.4 0.0 copy-done.1
  46.4 16.2 %fusion.6 = bf16[512,1024]{1,0:T(8,128)(2,1)} fusion(bf16[1024,4096]{1,0:T(8,128)(2,1)} %param.6, bf16[1024,4096]{1,0:T(8,128)(2,1)} %param.7, f32[1024]{0:T(1024)S(1)} %get-tuple-element.10, f32[1024]{0:T(1024)S(1)} %get-tuple-element.11, f32[1024]{0:T(1024)S(1)} %select_multiply_fusion, s32[512,1024]{1,0:T(8,128)S(1)} %copy-done.1), kind=kOutput, calls=%fused_computation.11 | convolution fusion | flops 9671016448 | bytes 19935232 | tf_op jit(solution)/shard_map/dot_general | solution.py:39
  62.6 0.0 all-reduce.3.cloned.1.call-update
  62.6 0.0 reduce-scatter.4.cloned.1.call-start
  62.7 83.6 %all-reduce.3.cloned.1.call-done = bf16[512,1024]{1,0:T(8,128)(2,1)} async-done(((bf16[512,1024]{1,0:T(8,128)(2,1)}), bf16[512,1024]{1,0:T(8,128)(2,1)}) %all-reduce.3.cloned.1.call-update) | async-done | bytes 1048592 | tf_op jit(solution)/shard_map/psum | solution.py:40
  146.3 4.8 %fusion = bf16[2048,512]{0,1:T(8,128)(2,1)S(1)} fusion(bf16[512,1024]{1,0:T(8,128)(2,1)} %all-reduce.3.cloned.1.call-done, bf16[1024,2048]{1,0:T(8,128)(2,1)} %param.8), kind=kOutput, calls=%fused_computation.4 | convolution fusion | flops 2148532224 | bytes 7340032 | tf_op jit(solution)/shard_map/dot_general | solution.py:12
  151.1 2.5 copy.10
  153.6 0.0 reduce-scatter.4.cloned.1.call-update
  153.7 62.8 %reduce-scatter.4.cloned.1.call-done = bf16[128,512]{1,0:T(8,128)(2,1)} async-done(((bf16[2048,512]{1,0:T(8,128)(2,1)}), bf16[128,512]{1,0:T(8,128)(2,1)}) %reduce-scatter.4.cloned.1.call-update) | async-done | bytes 131088
  216.4 1.0 copy.11
  217.4 0.2 multiply_reduce_fusion.2
  217.6 30.8 %psum.38 = f32[512]{0:T(512)S(1)} all-reduce(f32[512]{0:T(512)S(1)} %multiply_reduce_fusion.2), channel_id=1, replica_groups=mesh['sample'=8,'landmark'=16] {'landmark'}, use_global_device_ids=true, to_apply=%region_10.11 | all-reduce | flops 512 | bytes 4096 | tf_op jit(solution)/shard_map/psum | solution.py:48
  248.4 20.2 %psum.39 = f32[512]{0:T(512)S(1)} all-reduce(f32[512]{0:T(512)S(1)} %psum.38), channel_id=1, replica_groups=mesh['sample'=8,'landmark'=16] {'sample'}, use_global_device_ids=true, to_apply=%region_11.12 | all-reduce | flops 512 | bytes 4096 | tf_op jit(solution)/shard_map/psum | solution.py:48
  268.7 0.6 broadcast_multiply_fusion
  (1 shorter events, 0.0 us)
Async XLA Ops:
  7.2 139.1 %all-reduce.3.cloned.1.call-start = ((), (), s32[]{:S(2)}) async-start(), calls=%async_computation.1 | async-start | bytes 2097152 | tf_op jit(solution)/shard_map/psum | solution.py:40
  38.9 5.8 %copy-start = (bf16[1024,4096]{1,0:T(8,128)(2,1)S(1)}, bf16[1024,4096]{1,0:T(8,128)(2,1)}, u32[]{:S(2)}) copy-start(bf16[1024,4096]{1,0:T(8,128)(2,1)} %param.7) | copy-start | bytes 25165828
  44.7 1.7 copy-start.1
  62.6 153.8 %reduce-scatter.4.cloned.1.call-start = ((), (), s32[]{:S(2)}) async-start(), calls=%async_computation.2 | async-start | bytes 2228224
Sparse Core Ops, SparseCore 0:
  62.7 83.4 all-reduce.2
  153.8 62.5 reduce-scatter.3
